TPU v7x, 32 devices: a whole 2x2x4 slice. The times are simulated.
32 devices in a mesh: grp: 2 (over y), seq: 4 (over z), mdl: 2 (over x), sub: 2 (over core).
Axes of the slice: x: 2, y: 2, z: 4, core: 2. Of those that a mesh axis runs over, the one named last changes fastest.
Arguments:
- frames: bfloat16 [2048, 1280], P(('grp', 'seq', 'mdl')), parts along dimension 0, may hold values from -6 to 6
- audio_count: int32 [16], P(('grp', 'seq', 'mdl')), parts along dimension 0, may hold values from 1 to 127
- pos_ids: int32 [3, 2048], P(None, ('grp', 'seq', 'mdl')), parts along dimension 1, may hold values from 0 to 4095
- gain_audio: float32 [1280], replicated, may hold values from 0.1 to 1.9
- gain_video: float32 [1280], replicated, may hold values from 0.1 to 1.9
- audio_proj: bfloat16 [1280, 3584], P(('seq', 'mdl'), 'sub'), may hold values from -0.15625 to 0.15625
- video_proj: bfloat16 [1280, 3584], P(('seq', 'mdl'), 'sub'), may hold values from -0.15625 to 0.15625
- dest_device: int32 [2048], P(('grp', 'seq', 'mdl')), parts along dimension 0, may hold values from 0 to 7, as said below
- dest_slot: int32 [2048], P(('grp', 'seq', 'mdl')), parts along dimension 0, may hold values from 0 to 127, as said below
Outputs:
- lm_rows: bfloat16 [2048, 3584], P(('grp', 'seq', 'mdl'), 'sub'), parts along dimension 0
There are 2 independent parts, one for each index of `grp`. A program takes and returns all parts, laid end to end along the dimension named above; an argument that names none is the same for every part. Nothing has to cross between parts.
Inputs may be any that keep to these rules, and one draw needn't show every extreme that they name: The pairs (dest_device, dest_slot) name every row of the output exactly once. Each language-model shard receives exactly 128 tokens. At most 32 tokens of one source shard go to one language-model shard, and some pairs of shards reach 32. `dest_slot`: see dest_device.
All inputs are finite; a program needn't handle non-finite values.
Results may differ from a plain program's by a relative error of at most 0.0049.
Values may be sent and summed in bfloat16 or wider, within the bound.
A program may use at most 64 MiB of HBM per device.

v0:
```python
import jax
import jax.numpy as jnp
from jax import lax
from jax.sharding import PartitionSpec as P

HEAD = 128


def normalize(frames, audio_mask, gain_audio, gain_video):
    values = frames.astype(jnp.float32)
    mean_square = jnp.mean(values * values, axis=-1, keepdims=True)
    row_gain = jnp.where(audio_mask[:, None], gain_audio[None, :], gain_video[None, :])
    return (values * lax.rsqrt(mean_square + 1e-06) * row_gain).astype(jnp.bfloat16)


def rotate(values, positions):
    tok_rows = values.shape[0]
    half_size = HEAD // 2
    pair_index = jnp.arange(half_size, dtype=jnp.int32)[None, :]
    chosen = jnp.where(
        pair_index < HEAD // 8,
        positions[0][:, None],
        jnp.where(pair_index < HEAD * 5 // 16, positions[1][:, None], positions[2][:, None]),
    )
    exponent = -2.0 * jnp.arange(half_size).astype(jnp.float32) / HEAD
    inverse_freq = jnp.power(jnp.float32(1000000.0), exponent)
    angles = chosen.astype(jnp.float32) * inverse_freq[None, :]
    cosine = jnp.cos(angles)[:, None, :]
    sinus = jnp.sin(angles)[:, None, :]
    by_head = values.reshape(tok_rows, -1, HEAD)
    lower = by_head[:, :, :half_size]
    second = by_head[:, :, half_size:]
    turned = jnp.concatenate(
        [lower * cosine - second * sinus, second * cosine + lower * sinus], axis=-1
    )
    return turned.reshape(tok_rows, -1)


def embed_rows(normed, audio_mask, positions, audio_proj, video_proj):
    from_audio = jnp.dot(
        normed,
        lax.all_gather(audio_proj, ("seq", "mdl"), axis=0, tiled=True),
        preferred_element_type=jnp.float32,
    )
    from_video = jnp.dot(
        normed,
        lax.all_gather(video_proj, ("seq", "mdl"), axis=0, tiled=True),
        preferred_element_type=jnp.float32,
    )
    selected = jnp.where(audio_mask[:, None], from_audio, from_video)
    return rotate(selected, positions).astype(jnp.bfloat16)


def deliver(outbox, tag_rows):
    got_values, got_tags = (
        lax.all_to_all(outbox, ("seq", "mdl"), split_axis=0, concat_axis=0, tiled=True),
        lax.all_to_all(tag_rows, ("seq", "mdl"), split_axis=0, concat_axis=0, tiled=True),
    )
    return (got_values, got_tags)


def on_device(
    frames,
    audio_count,
    pos_ids,
    gain_audio,
    gain_video,
    audio_proj,
    video_proj,
    dest_device,
    dest_slot,
):
    tok_rows = frames.shape[0]
    audio_mask = jnp.arange(tok_rows, dtype=jnp.int32) < audio_count[0]
    peer_count = lax.axis_size(("seq", "mdl"))
    capacity = 2 * tok_rows // peer_count
    onehot = (dest_device[:, None] == jnp.arange(peer_count, dtype=jnp.int32)[None, :]).astype(
        jnp.int32
    )
    arrival = jnp.sum(jnp.cumsum(onehot, axis=0) * onehot, axis=1) - 1
    bucket = dest_device * capacity + arrival
    normed = normalize(frames, audio_mask, gain_audio, gain_video)
    features = normed.shape[1]
    described = jnp.concatenate(
        [pos_ids.T, audio_mask.astype(jnp.int32)[:, None], dest_slot[:, None]], axis=1
    )
    outbox = jnp.zeros((peer_count * capacity, features), jnp.bfloat16).at[bucket].set(normed)
    blank_tags = jnp.concatenate(
        [
            jnp.zeros((peer_count * capacity, 4), jnp.int32),
            jnp.full((peer_count * capacity, 1), tok_rows, jnp.int32),
        ],
        axis=1,
    )
    tag_rows = blank_tags.at[bucket].set(described)
    received, got_tags = deliver(outbox, tag_rows)
    arrived = got_tags[:, 4]
    placed = jnp.zeros((tok_rows, features), jnp.bfloat16).at[arrived].set(received, mode="drop")
    placed_tags = jnp.zeros((tok_rows, 5), jnp.int32).at[arrived].set(got_tags, mode="drop")
    return embed_rows(placed, placed_tags[:, 3] > 0, placed_tags[:, :3].T, audio_proj, video_proj)


def solution(mesh):
    in_specs = (
        P(("grp", "seq", "mdl"), None),
        P(("grp", "seq", "mdl")),
        P(None, ("grp", "seq", "mdl")),
        P(),
        P(),
        P(("seq", "mdl"), "sub"),
        P(("seq", "mdl"), "sub"),
        P(("grp", "seq", "mdl")),
        P(("grp", "seq", "mdl")),
    )
    out_specs = P(("grp", "seq", "mdl"), "sub")
    return jax.shard_map(
        on_device, mesh=mesh, in_specs=in_specs, out_specs=out_specs, check_vma=False
    )
```

profile of v0, /device:TPU:0, one launch (start us, length us, event | category | flops | bytes accessed | tf_op | source)
XLA Modules:
  0.0 190.9 jit_solution(18242663805615609553)
XLA Ops:
  6.5 0.7 all-gather.3.cloned.1.call-update
  7.3 0.7 all-gather.5.cloned.1.call-update
  8.7 0.7 pad_add_fusion
  9.4 0.1 copy.23
  9.5 0.9 copy.32
  10.4 0.7 fusion.12
  11.1 0.2 reduce_window_sum.11
  11.3 0.8 select_reduce_fusion
  12.1 0.7 compare_select_fusion.1
  12.8 0.9 scatter_fusion
  13.9 0.7 reshape.246
  14.6 7.3 %all-to-all-start = ((s32[8,1,160]{2,1,0:T(1,128)}), s32[8,1,160]{2,1,0:T(1,128)S(1)}, u32[]{:S(2)}, u32[]{:S(2)}) async-start(s32[8,1,160]{2,1,0:T(1,128)} %reshape.246), calls=%async_computation | async-start | bytes 16384 | tf_op jit(solution)/shard_map/all_to_all | solution.py:57
  21.9 1.1 fusion
  23.0 2.6 %scatter_custom_fusion.2 = bf16[256,1280]{1,0:T(8,128)(2,1)} fusion(s32[128]{0:T(128)S(1)} %compare_select_fusion.1, bf16[128,1280]{1,0:T(8,128)(2,1)} %param.9, f32[1280]{0:T(1024)} %param.13, f32[1280]{0:T(1024)} %param.12, f32[128]{0:T(128)S(1)} %add_rsqrt_fusion, bf16[]{:T(256)} %constant.7.clone.1, pred[128]{0:T(512)(128)(4,1)S(1)} %iota_compare_fusion.3), kind=kCustom, calls=%fused_computation.13 | custom fusion | flops 819200 | bytes 994306 | tf_op jit(solution)/shard_map/scatter | solution.py:87
  25.6 3.0 %all-to-all-done = s32[8,1,160]{2,1,0:T(1,128)S(1)} async-done(((s32[8,1,160]{2,1,0:T(1,128)}), s32[8,1,160]{2,1,0:T(1,128)S(1)}, u32[]{:S(2)}, u32[]{:S(2)}) %all-to-all-start) | async-done | bytes 5152 | tf_op jit(solution)/shard_map/all_to_all | solution.py:57
  28.6 3.5 %all-to-all-start.1 = ((bf16[8,32,1280]{2,1,0:T(8,128)(2,1)}), bf16[8,32,1280]{2,1,0:T(8,128)(2,1)S(1)}, u32[]{:S(2)}, u32[]{:S(2)}) async-start(bf16[8,32,1280]{2,1,0:T(8,128)(2,1)} %bitcast.5), calls=%async_computation.1 | async-start | bytes 1310720 | tf_op jit(solution)/shard_map/all_to_all | solution.py:56
  32.2 0.5 broadcast.164
  32.7 0.7 reduce.8
  33.5 0.1 copy.26
  33.7 1.2 scatter_custom_fusion.1
  34.9 0.2 fusion.13
  35.1 0.2 slice_reduce_fusion.2
  35.3 0.2 fusion.15
  35.5 21.6 %all-to-all-done.1 = bf16[8,32,1280]{2,1,0:T(8,128)(2,1)S(1)} async-done(((bf16[8,32,1280]{2,1,0:T(8,128)(2,1)}), bf16[8,32,1280]{2,1,0:T(8,128)(2,1)S(1)}, u32[]{:S(2)}, u32[]{:S(2)}) %all-to-all-start.1) | async-done | bytes 655392 | tf_op jit(solution)/shard_map/all_to_all | solution.py:56
  57.1 1.7 scatter_custom_fusion.3
  58.8 42.4 %all-gather.3.cloned.1.call-done = bf16[1280,1792]{1,0:T(8,128)(2,1)} async-done(((bf16[160,1792]{1,0:T(8,128)(2,1)}), bf16[1280,1792]{1,0:T(8,128)(2,1)}) %all-gather.3.cloned.1.call-update) | async-done | bytes 4587536 | tf_op jit(solution)/shard_map/all_gather | solution.py:42
  101.2 3.1 %fusion.18 = f32[128,1792]{1,0:T(8,128)S(1)} fusion(bf16[128,1280]{1,0:T(8,128)(2,1)S(1)} %scatter_custom_fusion.3, bf16[1280,1792]{1,0:T(8,128)(2,1)} %all-gather.3.cloned.1.call-done), kind=kOutput, calls=%fused_computation.44 | convolution fusion | flops 587202560 | bytes 5832704 | tf_op jit(solution)/shard_map/dot_general | solution.py:40
  104.3 75.2 %all-gather.5.cloned.1.call-done = bf16[1280,1792]{1,0:T(8,128)(2,1)} async-done(((bf16[160,1792]{1,0:T(8,128)(2,1)}), bf16[1280,1792]{1,0:T(8,128)(2,1)}) %all-gather.5.cloned.1.call-update) | async-done | bytes 4587536 | tf_op jit(solution)/shard_map/all_gather | solution.py:47
  179.5 3.1 %convolution_select_fusion = f32[128,1792]{1,0:T(8,128)S(1)} fusion(f32[128,1792]{1,0:T(8,128)S(1)} %fusion.18, bf16[128,1280]{1,0:T(8,128)(2,1)S(1)} %scatter_custom_fusion.3, bf16[1280,1792]{1,0:T(8,128)(2,1)} %all-gather.5.cloned.1.call-done, pred[128]{0:T(512)(128)(4,1)S(1)} %fusion.13), kind=kOutput, calls=%fused_computation.4 | convolution fusion | flops 587431936 | bytes 6750336 | tf_op jit(solution)/shard_map/dot_general | solution.py:45
  182.6 0.3 copy.27
  182.9 0.1 subtract_convert_fusion
  183.1 1.0 copy.28
  (14 shorter events, 0.4 us)
Async XLA Ops:
  6.5 94.7 %all-gather.3.cloned.1.call-start = ((), (), s32[]{:S(2)}) async-start(), calls=%async_computation.2 | async-start | bytes 5160960 | tf_op jit(solution)/shard_map/all_gather | solution.py:42
  7.3 172.3 %all-gather.5.cloned.1.call-start = ((), (), s32[]{:S(2)}) async-start(), calls=%async_computation.3 | async-start | bytes 5160960 | tf_op jit(solution)/shard_map/all_gather | solution.py:47
  14.6 14.0 %all-to-all-start = ((s32[8,1,160]{2,1,0:T(1,128)}), s32[8,1,160]{2,1,0:T(1,128)S(1)}, u32[]{:S(2)}, u32[]{:S(2)}) async-start(s32[8,1,160]{2,1,0:T(1,128)} %reshape.246), calls=%async_computation | async-start | bytes 16384 | tf_op jit(solution)/shard_map/all_to_all | solution.py:57
  28.6 28.5 %all-to-all-start.1 = ((bf16[8,32,1280]{2,1,0:T(8,128)(2,1)}), bf16[8,32,1280]{2,1,0:T(8,128)(2,1)S(1)}, u32[]{:S(2)}, u32[]{:S(2)}) async-start(bf16[8,32,1280]{2,1,0:T(8,128)(2,1)} %bitcast.5), calls=%async_computation.1 | async-start | bytes 1310720 | tf_op jit(solution)/shard_map/all_to_all | solution.py:56
Sparse Core Ops, SparseCore 0:
  9.5 91.6 all-gather.2
  103.4 76.0 all-gather.4
where the time goes:
time: 191 us
  waiting for transfers between devices  144 us (75%)
  between operations  14.2 us (7%)
  starting transfers between devices  10.9 us (6%)
  other arithmetic  8.09 us (4%)
  local copies, waits for them, and re-layouts  7.95 us (4%)
  matrix products  6.15 us (3%)
    all_gather x1, waiting for transfers between devices, embed_rows(): lax.all_gather(video_proj, ('seq', 'mdl'), axis=0, tiled=True)  75.2 us
    all_gather x1, waiting for transfers between devices, embed_rows(): lax.all_gather(audio_proj, ('seq', 'mdl'), axis=0, tiled=True)  42.4 us
    all_to_all x1, waiting for transfers between devices, deliver(): lax.all_to_all(outbox, ('seq', 'mdl'), split_axis=0, concat_axis=0, tiled...  21.6 us
    all_to_all x1, starting transfers between devices, deliver(): lax.all_to_all(tag_rows, ('seq', 'mdl'), split_axis=0, concat_axis=0, til...  7.28 us
  transfers between devices with their start and end apart: 4, of which 4 were waited for; matrix products, arithmetic and copies ran while one was open for 9% of the time, Pallas kernels for 0%

commit v1 on v0

--- a/solution.py
+++ b/solution.py
@@ -1,9 +1,15 @@
+import functools
+
 import jax
 import jax.numpy as jnp
 from jax import lax
+from jax.experimental import pallas as pl
+from jax.experimental.pallas import tpu as pltpu
 from jax.sharding import PartitionSpec as P
 
 HEAD = 128
+META = 16
+MESH = pl.DeviceIdType.MESH
 
 
 def normalize(frames, audio_mask, gain_audio, gain_video):
@@ -11,6 +17,11 @@
     mean_square = jnp.mean(values * values, axis=-1, keepdims=True)
     row_gain = jnp.where(audio_mask[:, None], gain_audio[None, :], gain_video[None, :])
     return (values * lax.rsqrt(mean_square + 1e-06) * row_gain).astype(jnp.bfloat16)
+
+
+def inverse_frequencies():
+    exponent = -2.0 * jnp.arange(HEAD // 2).astype(jnp.float32) / HEAD
+    return jnp.power(jnp.float32(1000000.0), exponent)
 
 
 def rotate(values, positions):
@@ -22,9 +33,7 @@
         positions[0][:, None],
         jnp.where(pair_index < HEAD * 5 // 16, positions[1][:, None], positions[2][:, None]),
     )
-    exponent = -2.0 * jnp.arange(half_size).astype(jnp.float32) / HEAD
-    inverse_freq = jnp.power(jnp.float32(1000000.0), exponent)
-    angles = chosen.astype(jnp.float32) * inverse_freq[None, :]
+    angles = chosen.astype(jnp.float32) * inverse_frequencies()[None, :]
     cosine = jnp.cos(angles)[:, None, :]
     sinus = jnp.sin(angles)[:, None, :]
     by_head = values.reshape(tok_rows, -1, HEAD)
@@ -51,24 +60,8 @@
     return rotate(selected, positions).astype(jnp.bfloat16)
 
 
-def deliver(outbox, tag_rows):
-    got_values, got_tags = (
-        lax.all_to_all(outbox, ("seq", "mdl"), split_axis=0, concat_axis=0, tiled=True),
-        lax.all_to_all(tag_rows, ("seq", "mdl"), split_axis=0, concat_axis=0, tiled=True),
-    )
-    return (got_values, got_tags)
-
-
-def on_device(
-    frames,
-    audio_count,
-    pos_ids,
-    gain_audio,
-    gain_video,
-    audio_proj,
-    video_proj,
-    dest_device,
-    dest_slot,
+def gathered_plan(
+    frames, audio_count, pos_ids, gain_audio, gain_video, audio_proj, video_proj, dest_device, dest_slot
 ):
     tok_rows = frames.shape[0]
     audio_mask = jnp.arange(tok_rows, dtype=jnp.int32) < audio_count[0]
@@ -93,11 +86,355 @@
         axis=1,
     )
     tag_rows = blank_tags.at[bucket].set(described)
-    received, got_tags = deliver(outbox, tag_rows)
+    received = lax.all_to_all(outbox, ("seq", "mdl"), split_axis=0, concat_axis=0, tiled=True)
+    got_tags = lax.all_to_all(tag_rows, ("seq", "mdl"), split_axis=0, concat_axis=0, tiled=True)
     arrived = got_tags[:, 4]
     placed = jnp.zeros((tok_rows, features), jnp.bfloat16).at[arrived].set(received, mode="drop")
     placed_tags = jnp.zeros((tok_rows, 5), jnp.int32).at[arrived].set(got_tags, mode="drop")
     return embed_rows(placed, placed_tags[:, 3] > 0, placed_tags[:, :3].T, audio_proj, video_proj)
+
+
+def kernel(
+    n_seq,
+    chunk,
+    early,
+    count_ref,
+    frames_ref,
+    pos_ref,
+    dev_ref,
+    slot_ref,
+    gain_a_ref,
+    gain_v_ref,
+    freq_ref,
+    audio_hbm,
+    video_hbm,
+    out_ref,
+    xbuf,
+    stage,
+    meta,
+    hot,
+    lhs,
+    weights,
+    outbox,
+    inbox,
+    own,
+    turn,
+    x1_send,
+    x1_recv,
+    m1_send,
+    m1_recv,
+    x2_sem,
+    m2_sem,
+    x3_sem,
+    w_send,
+    w_recv,
+    w_own,
+    p_send,
+    p_recv,
+):
+    z = lax.axis_index("seq")
+    x = lax.axis_index("mdl")
+    core = lax.axis_index("sub")
+    tok, features = frames_ref.shape
+    deep = audio_hbm.shape[0]
+    width = features // n_seq
+    chunks = audio_hbm.shape[1] // chunk
+    part = tok // 2
+    mine = pl.ds(pl.multiple_of(core * part, part), part)
+
+    def seq_peer(step):
+        return lax.rem(z + step, n_seq)
+
+    barrier = pltpu.get_barrier_semaphore()
+    for step in range(1, n_seq):
+        pl.semaphore_signal(barrier, inc=1, device_id={"seq": seq_peer(step)}, device_id_type=MESH)
+    pl.semaphore_signal(barrier, inc=1, device_id={"mdl": 1 - x}, device_id_type=MESH)
+    pl.semaphore_signal(barrier, inc=1, device_id={"sub": 1 - core}, device_id_type=MESH)
+
+    def weight_rows(kind):
+        return pl.ds(pl.multiple_of(kind * width + x * deep, 16), deep)
+
+    own_weights = [
+        pltpu.make_async_copy(ref, weights.at[weight_rows(kind)], w_own.at[kind])
+        for kind, ref in enumerate((audio_hbm, video_hbm))
+    ]
+    for copy in own_weights:
+        copy.start()
+
+    def weight_copy(kind, c):
+        ref = (audio_hbm, video_hbm)[kind]
+        cols = pl.ds(pl.multiple_of(c * chunk, chunk), chunk)
+        return pltpu.make_async_remote_copy(
+            src_ref=ref.at[:, cols],
+            dst_ref=weights.at[weight_rows(kind), cols],
+            send_sem=w_send.at[kind, c],
+            recv_sem=w_recv.at[kind, c],
+            device_id={"mdl": 1 - x},
+            device_id_type=MESH,
+        )
+
+    def weight_arrival(kind, c):
+        ref = (audio_hbm, video_hbm)[kind]
+        cols = pl.ds(pl.multiple_of(c * chunk, chunk), chunk)
+        rows = pl.ds(pl.multiple_of(kind * width + (1 - x) * deep, 16), deep)
+        return pltpu.make_async_remote_copy(
+            src_ref=ref.at[:, cols],
+            dst_ref=weights.at[rows, cols],
+            send_sem=w_send.at[kind, c],
+            recv_sem=w_recv.at[kind, c],
+            device_id={"mdl": 1 - x},
+            device_id_type=MESH,
+        )
+
+    count = count_ref[0]
+    values = frames_ref[mine, :].astype(jnp.float32)
+    mean_square = jnp.mean(values * values, axis=-1, keepdims=True)
+    token = lax.broadcasted_iota(jnp.int32, (part, features), 0) + core * part
+    gain = jnp.where(token < count, gain_a_ref[...], gain_v_ref[...])
+    normed = (values * lax.rsqrt(mean_square + 1e-06) * gain).astype(jnp.bfloat16)
+    for target in range(n_seq):
+        stage[target] = normed[:, target * width : (target + 1) * width]
+
+    lane = lax.broadcasted_iota(jnp.int32, (META, tok), 1)
+    row = lax.broadcasted_iota(jnp.int32, (META, tok), 0)
+    device = dev_ref[...]
+    target_seq = device // 2
+    lines = [pos_ref[i : i + 1, :] >> 6 for i in range(3)]
+    lines += [pos_ref[i : i + 1, :] & 63 for i in range(3)]
+    lines += [jnp.where(lane[0:1, :] < count, 1, 0)]
+    lines += [target_seq, device - target_seq * 2, slot_ref[...]]
+    table = jnp.zeros((META, tok), jnp.int32)
+    for i, line in enumerate(lines):
+        table = jnp.where(row == i, line, table)
+    meta[x, z] = table.astype(jnp.float32)
+
+    pl.semaphore_wait(barrier, n_seq + 1)
+
+    def x1_copy(step, source):
+        return pltpu.make_async_remote_copy(
+            src_ref=stage.at[seq_peer(step)],
+            dst_ref=xbuf.at[x, source, mine],
+            send_sem=x1_send.at[step],
+            recv_sem=x1_recv.at[step],
+            device_id={"seq": seq_peer(step)},
+            device_id_type=MESH,
+        )
+
+    def m1_copy(step, source):
+        return pltpu.make_async_remote_copy(
+            src_ref=meta.at[x, z],
+            dst_ref=meta.at[x, source],
+            send_sem=m1_send.at[step],
+            recv_sem=m1_recv.at[step],
+            device_id={"seq": seq_peer(step)},
+            device_id_type=MESH,
+        )
+
+    for step in range(1, n_seq):
+        x1_copy(step, z).start()
+        m1_copy(step, z).start()
+    for c in range(early):
+        for kind in range(2):
+            weight_copy(kind, c).start()
+    xbuf[x, z, mine, :] = stage[z]
+    for step in range(1, n_seq):
+        x1_copy(step, seq_peer(n_seq - step)).wait_recv()
+        m1_copy(step, seq_peer(n_seq - step)).wait_recv()
+
+    def x2_copy(column):
+        return pltpu.make_async_remote_copy(
+            src_ref=xbuf.at[x, :, mine],
+            dst_ref=xbuf.at[column, :, mine],
+            send_sem=x2_sem.at[0],
+            recv_sem=x2_sem.at[1],
+            device_id={"mdl": 1 - x},
+            device_id_type=MESH,
+        )
+
+    def m2_copy(column):
+        return pltpu.make_async_remote_copy(
+            src_ref=meta.at[x],
+            dst_ref=meta.at[column],
+            send_sem=m2_sem.at[0],
+            recv_sem=m2_sem.at[1],
+            device_id={"mdl": 1 - x},
+            device_id_type=MESH,
+        )
+
+    def x3_copy(column, half):
+        rows = pl.ds(pl.multiple_of(half * part, part), part)
+        return pltpu.make_async_remote_copy(
+            src_ref=xbuf.at[column, :, mine],
+            dst_ref=xbuf.at[column, :, rows],
+            send_sem=x3_sem.at[0, column],
+            recv_sem=x3_sem.at[1, column],
+            device_id={"sub": 1 - core},
+            device_id_type=MESH,
+        )
+
+    m2_copy(x).start()
+    x2_copy(x).start()
+    for c in range(early, chunks):
+        for kind in range(2):
+            weight_copy(kind, c).start()
+    x3_copy(x, core).start()
+    m2_copy(1 - x).wait_recv()
+
+    rows = lax.broadcasted_iota(jnp.int32, (n_seq * tok, tok), 0)
+    facts = jnp.zeros((n_seq * tok, META), jnp.float32)
+    for k in range(2 * n_seq):
+        about = meta[k // n_seq, k % n_seq]
+        ints = about.astype(jnp.int32)
+        ahead = ints[7:8, :] - z
+        ahead = jnp.where(ahead < 0, ahead + n_seq, ahead)
+        key = jnp.where(ints[8:9, :] == x, ahead * tok + ints[9:10, :], -1)
+        piece = jnp.where(rows == key, 1.0, 0.0).astype(jnp.bfloat16)
+        hot[:, k * tok : (k + 1) * tok] = piece
+        facts += lax.dot_general(
+            piece, about.astype(jnp.bfloat16), (((1,), (1,)), ((), ())), preferred_element_type=jnp.float32
+        )
+
+    lanes = lax.broadcasted_iota(jnp.int32, (tok, HEAD), 1)
+    pair = jnp.where(lanes < HEAD // 2, lanes, lanes - HEAD // 2)
+    place = [facts[:tok, i : i + 1] * 64.0 + facts[:tok, i + 3 : i + 4] for i in range(3)]
+    chosen = jnp.where(pair < HEAD // 8, place[0], jnp.where(pair < HEAD * 5 // 16, place[1], place[2]))
+    angles = chosen * freq_ref[...]
+    turn[0] = jnp.cos(angles)
+    sinus = jnp.sin(angles)
+    turn[1] = jnp.where(lanes < HEAD // 2, -sinus, sinus)
+
+    x2_copy(1 - x).wait_recv()
+    x3_copy(1 - x, core).start()
+    for column in range(2):
+        x3_copy(column, 1 - core).wait_recv()
+
+    everyone = xbuf[...].reshape(2 * n_seq * tok, width)
+    sorted_rows = jnp.dot(hot[...], everyone, preferred_element_type=jnp.float32)
+    is_audio = facts[:, 6:7] > 0.5
+    lhs[:, :width] = jnp.where(is_audio, sorted_rows, 0.0).astype(jnp.bfloat16)
+    lhs[:, width:] = jnp.where(is_audio, 0.0, sorted_rows).astype(jnp.bfloat16)
+
+    for copy in own_weights:
+        copy.wait()
+
+    def part_copy(step, c):
+        return pltpu.make_async_remote_copy(
+            src_ref=outbox.at[step - 1, c],
+            dst_ref=inbox.at[step - 1, c],
+            send_sem=p_send.at[step - 1, c],
+            recv_sem=p_recv.at[step - 1, c],
+            device_id={"seq": seq_peer(step)},
+            device_id_type=MESH,
+        )
+
+    def multiply(c, carry):
+        for kind in range(2):
+            weight_arrival(kind, c).wait_recv()
+        cols = pl.ds(pl.multiple_of(c * chunk, chunk), chunk)
+        product = jnp.dot(lhs[...], weights[:, cols], preferred_element_type=jnp.float32)
+        for step in range(1, n_seq):
+            outbox[step - 1, c] = product[step * tok : (step + 1) * tok, :].astype(jnp.bfloat16)
+        for step in range(1, n_seq):
+            part_copy(step, c).start()
+        own[c] = product[:tok, :]
+        return carry
+
+    lax.fori_loop(0, chunks, multiply, 0)
+
+    def finish(c, carry):
+        for step in range(1, n_seq):
+            part_copy(step, c).wait_recv()
+        total = own[c]
+        for step in range(1, n_seq):
+            total += inbox[step - 1, c].astype(jnp.float32)
+        for h in range(chunk // HEAD):
+            head = total[:, h * HEAD : (h + 1) * HEAD]
+            turned = head * turn[0] + pltpu.roll(head, HEAD // 2, 1) * turn[1]
+            at = pl.ds(pl.multiple_of(c * chunk + h * HEAD, HEAD), HEAD)
+            out_ref[:, at] = turned.astype(out_ref.dtype)
+        return carry
+
+    lax.fori_loop(0, chunks, finish, 0)
+
+    for step in range(1, n_seq):
+        x1_copy(step, z).wait_send()
+        m1_copy(step, z).wait_send()
+    x2_copy(x).wait_send()
+    m2_copy(x).wait_send()
+    for column in range(2):
+        x3_copy(column, core).wait_send()
+
+    def drain(c, carry):
+        for kind in range(2):
+            weight_copy(kind, c).wait_send()
+        for step in range(1, n_seq):
+            part_copy(step, c).wait_send()
+        return carry
+
+    lax.fori_loop(0, chunks, drain, 0)
+
+
+def exchanged_plan(
+    frames, audio_count, pos_ids, gain_audio, gain_video, audio_proj, video_proj, dest_device, dest_slot
+):
+    n_seq = lax.axis_size("seq")
+    tok, features = frames.shape
+    deep, columns = audio_proj.shape
+    width = features // n_seq
+    chunk = next(k for k in (2 * HEAD, HEAD) if columns % k == 0)
+    chunks = columns // chunk
+    early = min(2, chunks)
+    freq = inverse_frequencies()
+    freq = jnp.concatenate([freq, freq])[None, :]
+    vmem = pl.BlockSpec(memory_space=pltpu.VMEM)
+    smem = pl.BlockSpec(memory_space=pltpu.SMEM)
+    anywhere = pl.BlockSpec(memory_space=pl.ANY)
+    dma = pltpu.SemaphoreType.DMA
+    bf16, f32 = jnp.bfloat16, jnp.float32
+    return pl.pallas_call(
+        functools.partial(kernel, n_seq, chunk, early),
+        out_shape=jax.ShapeDtypeStruct((tok, columns), bf16),
+        in_specs=[smem] + [vmem] * 7 + [anywhere] * 2,
+        out_specs=vmem,
+        scratch_shapes=[
+            pltpu.VMEM((2, n_seq, tok, width), bf16),
+            pltpu.VMEM((n_seq, tok // 2, width), bf16),
+            pltpu.VMEM((2, n_seq, META, tok), f32),
+            pltpu.VMEM((n_seq * tok, 2 * n_seq * tok), bf16),
+            pltpu.VMEM((n_seq * tok, 2 * width), bf16),
+            pltpu.VMEM((2 * width, columns), bf16),
+            pltpu.VMEM((n_seq - 1, chunks, tok, chunk), bf16),
+            pltpu.VMEM((n_seq - 1, chunks, tok, chunk), bf16),
+            pltpu.VMEM((chunks, tok, chunk), f32),
+            pltpu.VMEM((2, tok, HEAD), f32),
+            dma((n_seq,)),
+            dma((n_seq,)),
+            dma((n_seq,)),
+            dma((n_seq,)),
+            dma((2,)),
+            dma((2,)),
+            dma((2, 2)),
+            dma((2, chunks)),
+            dma((2, chunks)),
+            dma((2,)),
+            dma((n_seq - 1, chunks)),
+            dma((n_seq - 1, chunks)),
+        ],
+        compiler_params=pltpu.CompilerParams(
+            collective_id=0, has_side_effects=True, vmem_limit_bytes=48 * 1024 * 1024
+        ),
+    )(
+        audio_count,
+        frames,
+        pos_ids,
+        dest_device[None, :],
+        dest_slot[None, :],
+        gain_audio[None, :],
+        gain_video[None, :],
+        freq,
+        audio_proj,
+        video_proj,
+    )
 
 
 def solution(mesh):
@@ -113,6 +450,6 @@
         P(("grp", "seq", "mdl")),
     )
     out_specs = P(("grp", "seq", "mdl"), "sub")
-    return jax.shard_map(
-        on_device, mesh=mesh, in_specs=in_specs, out_specs=out_specs, check_vma=False
-    )
+    paired = mesh.shape["mdl"] == 2 and mesh.shape["sub"] == 2
+    plan = exchanged_plan if paired else gathered_plan
+    return jax.shard_map(plan, mesh=mesh, in_specs=in_specs, out_specs=out_specs, check_vma=False)

time: 191 us -> 68.8 us (0.36)
  waiting for transfers between devices: 144 us -> 0 us
  Pallas kernels: 0 us -> 61.8 us
  between operations: 14.2 us -> 0.7 us
  starting transfers between devices: 10.9 us -> 0 us
  other arithmetic: 8.09 us -> 0.08 us
  matrix products: 6.15 us -> 0 us
  local copies, waits for them, and re-layouts: 7.95 us -> 5.14 us
    all_gather x2 -> x0, waiting for transfers between devices: 118 us -> none  [the longest x1 75.2 us: embed_rows(): lax.all_gather(video_proj, ('seq', 'mdl'), axis=0, tiled=True)]
    pallas_call x0 -> x1, Pallas kernels: none -> 61.8 us  [exchanged_plan(): pl.pallas_call(functools.partial(kernel, n_seq, chunk, early), out_shape=...]
    all_to_all x2 -> x0, waiting for transfers between devices: 24.6 us -> none  [the longest x1 21.6 us: deliver(): lax.all_to_all(outbox, ('seq', 'mdl'), split_axis=0, concat_axis=0, tiled...]
    all_to_all x2 -> x0, starting transfers between devices: 10.8 us -> none  [the longest x1 7.28 us: deliver(): lax.all_to_all(tag_rows, ('seq', 'mdl'), split_axis=0, concat_axis=0, til...]
    dot_general x2 -> x0, matrix products: 6.15 us -> none  [the longest x1 3.08 us: embed_rows(): jnp.dot(normed, lax.all_gather(video_proj, ('seq', 'mdl'), axis=0, tiled=...]
    scatter x3 -> x0, local copies, waits for them, and re-layouts: 3.84 us -> none  [the longest x1 1.73 us: on_device(): jnp.zeros((tok_rows, features), jnp.bfloat16).at[arrived]]
    unnamed x3 -> x17, local copies, waits for them, and re-layouts: 1.67 us -> 5.13 us
    scatter x1 -> x0, other arithmetic: 2.59 us -> none  [on_device(): jnp.zeros((peer_count * capacity, features), jnp.bfloat16).at[bucket]]
  transfers between devices with their start and end apart: 4 -> 0, of which waited for: 4 -> 0; matrix products, arithmetic and copies ran while one was open for 9% -> 0% of each run, Pallas kernels for 0% -> 0%
where the time goes in v1:
time: 68.8 us; the launch traced here: 67.7 us
  Pallas kernels  61.8 us (90%)
  local copies, waits for them, and re-layouts  5.14 us (7%)
  between operations  0.7 us (1%)
    pallas_call x1, Pallas kernels, exchanged_plan(): pl.pallas_call(functools.partial(kernel, n_seq, chunk, early), out_shape=...  61.8 us
    unnamed x17, local copies, waits for them, and re-layouts  5.13 us

profile of v1, /device:TPU:0, one launch (start us, length us, event | category | flops | bytes accessed | tf_op | source)
XLA Modules:
  0.0 67.7 jit_solution(15541160072816849328)
XLA Ops:
  0.0 0.0 copy-start.6
  0.7 0.0 copy-start.7
  0.7 0.1 maximum_bitcast_fusion.freq_ref
  0.8 0.0 copy-done.6
  0.8 0.6 copy-done.7
  1.4 0.0 copy-start.3
  1.4 0.0 copy-start.4
  1.4 0.0 copy-start.5
  1.4 0.7 copy-done.3
  2.0 0.0 copy-done.4
  2.1 0.0 copy-done.5
  2.1 0.0 copy-start
  2.1 1.1 %copy-done = bf16[160,1792]{1,0:T(8,128)(2,1)S(1)} copy-done((bf16[160,1792]{1,0:T(8,128)(2,1)S(1)}, bf16[160,1792]{1,0:T(8,128)(2,1)}, u32[]{:S(2)}) %copy-start) | copy-done | bytes 573464
  3.1 0.0 copy-start.1
  3.1 1.1 %copy-done.1 = bf16[160,1792]{1,0:T(8,128)(2,1)S(1)} copy-done((bf16[160,1792]{1,0:T(8,128)(2,1)S(1)}, bf16[160,1792]{1,0:T(8,128)(2,1)}, u32[]{:S(2)}) %copy-start.1) | copy-done | bytes 573464
  4.2 0.0 copy-start.2
  4.2 1.0 %copy-done.2 = bf16[128,1280]{1,0:T(8,128)(2,1)S(1)} copy-done((bf16[128,1280]{1,0:T(8,128)(2,1)S(1)}, bf16[128,1280]{1,0:T(8,128)(2,1)}, u32[]{:S(2)}) %copy-start.2) | copy-done | bytes 327704
  5.1 61.8 %shard_map.91 = bf16[128,1792]{1,0:T(8,128)(2,1)S(1)} custom-call(s32[1]{0:T(128)S(6)} %copy.11.count_ref, bf16[128,1280]{1,0:T(8,128)(2,1)S(1)} %copy-done.2, s32[3,128]{1,0:T(4,128)S(1)} %copy-done.3, s32[1,128]{1,0:T(1,128)S(1)} %bitcast.4, s32[1,128]{1,0:T(1,128)S(1)} %bitcast.5, f32[1,1280]{1,0:T(1,128)S(1)} %broadcast_in_dim.17.gain_a_ref, ...), custom_call_target="tpu_custom_call" | custom-call | tf_op jit(solution)/shard_map/pallas_call | solution.py:394
  66.9 0.8 %copy.12 = bf16[128,1792]{1,0:T(8,128)(2,1)} copy(bf16[128,1792]{1,0:T(8,128)(2,1)S(1)} %shard_map.91) | data formatting | bytes 917504
  (3 shorter events, 0.0 us)
Async XLA Ops:
  0.0 0.8 %copy-start.6 = (f32[1280]{0:T(1024)S(1)}, f32[1280]{0:T(1024)}, u32[]{:S(2)}) copy-start(f32[1280]{0:T(1024)} %param.12) | copy-start | bytes 15364
  0.7 0.7 %copy-start.7 = (f32[1280]{0:T(1024)S(1)}, f32[1280]{0:T(1024)}, u32[]{:S(2)}) copy-start(f32[1280]{0:T(1024)} %param.13) | copy-start | bytes 15364
  1.4 0.7 %copy-start.3 = (s32[3,128]{1,0:T(4,128)S(1)}, s32[3,128]{1,0:T(4,128)}, u32[]{:S(2)}) copy-start(s32[3,128]{1,0:T(4,128)} %pos_ref.1) | copy-start | bytes 4612
  1.4 0.7 %copy-start.4 = (s32[128]{0:T(128)S(1)}, s32[128]{0:T(128)}, u32[]{:S(2)}) copy-start(s32[128]{0:T(128)} %param.16) | copy-start | bytes 1540
  1.4 0.7 %copy-start.5 = (s32[128]{0:T(128)S(1)}, s32[128]{0:T(128)}, u32[]{:S(2)}) copy-start(s32[128]{0:T(128)} %param.17) | copy-start | bytes 1540
  2.1 1.1 %copy-start = (bf16[160,1792]{1,0:T(8,128)(2,1)S(1)}, bf16[160,1792]{1,0:T(8,128)(2,1)}, u32[]{:S(2)}) copy-start(bf16[160,1792]{1,0:T(8,128)(2,1)} %audio_hbm.1) | copy-start | bytes 1720324
  3.1 1.1 %copy-start.1 = (bf16[160,1792]{1,0:T(8,128)(2,1)S(1)}, bf16[160,1792]{1,0:T(8,128)(2,1)}, u32[]{:S(2)}) copy-start(bf16[160,1792]{1,0:T(8,128)(2,1)} %video_hbm.1) | copy-start | bytes 1720324
  4.2 1.0 %copy-start.2 = (bf16[128,1280]{1,0:T(8,128)(2,1)S(1)}, bf16[128,1280]{1,0:T(8,128)(2,1)}, u32[]{:S(2)}) copy-start(bf16[128,1280]{1,0:T(8,128)(2,1)} %frames_ref.1) | copy-start | bytes 983044

commit v2 on v1

v2 whole, which is shorter than its diff:
```python
import functools

import jax
import jax.numpy as jnp
from jax import lax
from jax.experimental import pallas as pl
from jax.experimental.pallas import tpu as pltpu
from jax.sharding import PartitionSpec as P

HEAD = 128
META = 16
MESH = pl.DeviceIdType.MESH


def normalize(frames, audio_mask, gain_audio, gain_video):
    values = frames.astype(jnp.float32)
    mean_square = jnp.mean(values * values, axis=-1, keepdims=True)
    row_gain = jnp.where(audio_mask[:, None], gain_audio[None, :], gain_video[None, :])
    return (values * lax.rsqrt(mean_square + 1e-06) * row_gain).astype(jnp.bfloat16)


def inverse_frequencies():
    exponent = -2.0 * jnp.arange(HEAD // 2).astype(jnp.float32) / HEAD
    return jnp.power(jnp.float32(1000000.0), exponent)


def rotate(values, positions):
    tok_rows = values.shape[0]
    half_size = HEAD // 2
    pair_index = jnp.arange(half_size, dtype=jnp.int32)[None, :]
    chosen = jnp.where(
        pair_index < HEAD // 8,
        positions[0][:, None],
        jnp.where(pair_index < HEAD * 5 // 16, positions[1][:, None], positions[2][:, None]),
    )
    angles = chosen.astype(jnp.float32) * inverse_frequencies()[None, :]
    cosine = jnp.cos(angles)[:, None, :]
    sinus = jnp.sin(angles)[:, None, :]
    by_head = values.reshape(tok_rows, -1, HEAD)
    lower = by_head[:, :, :half_size]
    second = by_head[:, :, half_size:]
    turned = jnp.concatenate(
        [lower * cosine - second * sinus, second * cosine + lower * sinus], axis=-1
    )
    return turned.reshape(tok_rows, -1)


def embed_rows(normed, audio_mask, positions, audio_proj, video_proj):
    from_audio = jnp.dot(
        normed,
        lax.all_gather(audio_proj, ("seq", "mdl"), axis=0, tiled=True),
        preferred_element_type=jnp.float32,
    )
    from_video = jnp.dot(
        normed,
        lax.all_gather(video_proj, ("seq", "mdl"), axis=0, tiled=True),
        preferred_element_type=jnp.float32,
    )
    selected = jnp.where(audio_mask[:, None], from_audio, from_video)
    return rotate(selected, positions).astype(jnp.bfloat16)


def gathered_plan(
    frames, audio_count, pos_ids, gain_audio, gain_video, audio_proj, video_proj, dest_device, dest_slot
):
    tok_rows = frames.shape[0]
    audio_mask = jnp.arange(tok_rows, dtype=jnp.int32) < audio_count[0]
    peer_count = lax.axis_size(("seq", "mdl"))
    capacity = 2 * tok_rows // peer_count
    onehot = (dest_device[:, None] == jnp.arange(peer_count, dtype=jnp.int32)[None, :]).astype(
        jnp.int32
    )
    arrival = jnp.sum(jnp.cumsum(onehot, axis=0) * onehot, axis=1) - 1
    bucket = dest_device * capacity + arrival
    normed = normalize(frames, audio_mask, gain_audio, gain_video)
    features = normed.shape[1]
    described = jnp.concatenate(
        [pos_ids.T, audio_mask.astype(jnp.int32)[:, None], dest_slot[:, None]], axis=1
    )
    outbox = jnp.zeros((peer_count * capacity, features), jnp.bfloat16).at[bucket].set(normed)
    blank_tags = jnp.concatenate(
        [
            jnp.zeros((peer_count * capacity, 4), jnp.int32),
            jnp.full((peer_count * capacity, 1), tok_rows, jnp.int32),
        ],
        axis=1,
    )
    tag_rows = blank_tags.at[bucket].set(described)
    received = lax.all_to_all(outbox, ("seq", "mdl"), split_axis=0, concat_axis=0, tiled=True)
    got_tags = lax.all_to_all(tag_rows, ("seq", "mdl"), split_axis=0, concat_axis=0, tiled=True)
    arrived = got_tags[:, 4]
    placed = jnp.zeros((tok_rows, features), jnp.bfloat16).at[arrived].set(received, mode="drop")
    placed_tags = jnp.zeros((tok_rows, 5), jnp.int32).at[arrived].set(got_tags, mode="drop")
    return embed_rows(placed, placed_tags[:, 3] > 0, placed_tags[:, :3].T, audio_proj, video_proj)


def kernel(
    chunk,
    early,
    count_hbm,
    frames_hbm,
    pos_hbm,
    dev_hbm,
    slot_hbm,
    gain_a_hbm,
    gain_v_hbm,
    freq_ref,
    audio_hbm,
    video_hbm,
    out_ref,
    count_ref,
    frames_ref,
    pos_ref,
    dev_ref,
    slot_ref,
    gain_a_ref,
    gain_v_ref,
    xbuf,
    stage,
    meta,
    hot,
    lhs,
    weights,
    outbox,
    inbox,
    own,
    far,
    turn,
    in_sem,
    x1_send,
    x1_recv,
    m1_send,
    m1_recv,
    x2_send,
    x2_recv,
    m2_send,
    m2_recv,
    x3_send,
    x3_recv,
    w_send,
    w_recv,
    w_own,
    p_send,
    p_recv,
):
    n_seq = 4
    z = lax.axis_index("seq")
    x = lax.axis_index("mdl")
    core = lax.axis_index("sub")
    features = frames_hbm.shape[1]
    tok = frames_hbm.shape[0]
    deep = audio_hbm.shape[0]
    width = features // n_seq
    chunks = audio_hbm.shape[1] // chunk
    part = tok // 2
    mine = pl.ds(pl.multiple_of(core * part, part), part)
    inner = jnp.logical_or(z == 1, z == 2)
    peers = (z, z + 1 - 2 * lax.rem(z, 2), lax.rem(z + 2, n_seq), n_seq - 1 - z)

    loads = [
        pltpu.make_async_copy(src, dst, in_sem.at[i])
        for i, (src, dst) in enumerate(
            (
                (frames_hbm.at[mine], frames_ref),
                (gain_a_hbm, gain_a_ref),
                (gain_v_hbm, gain_v_ref),
                (count_hbm, count_ref),
                (pos_hbm, pos_ref),
                (dev_hbm, dev_ref),
                (slot_hbm, slot_ref),
            )
        )
    ]
    for copy in loads:
        copy.start()

    barrier = pltpu.get_barrier_semaphore()
    for q in range(1, n_seq):
        pl.semaphore_signal(barrier, inc=1, device_id={"seq": peers[q]}, device_id_type=MESH)
    pl.semaphore_signal(barrier, inc=1, device_id={"mdl": 1 - x}, device_id_type=MESH)
    pl.semaphore_signal(barrier, inc=1, device_id={"sub": 1 - core}, device_id_type=MESH)

    def weight_rows(kind, column):
        return pl.ds(pl.multiple_of(kind * width + column * deep, 16), deep)

    own_weights = [
        pltpu.make_async_copy(ref, weights.at[weight_rows(kind, x)], w_own.at[kind])
        for kind, ref in enumerate((audio_hbm, video_hbm))
    ]
    for copy in own_weights:
        copy.start()

    def weight_copy(kind, c, column):
        cols = pl.ds(pl.multiple_of(c * chunk, chunk), chunk)
        return pltpu.make_async_remote_copy(
            src_ref=(audio_hbm, video_hbm)[kind].at[:, cols],
            dst_ref=weights.at[weight_rows(kind, column), cols],
            send_sem=w_send.at[kind, c],
            recv_sem=w_recv.at[kind, c],
            device_id={"mdl": 1 - x},
            device_id_type=MESH,
        )

    for copy in loads:
        copy.wait()
    count = count_ref[0]
    lane = lax.broadcasted_iota(jnp.int32, (META, tok), 1)
    row = lax.broadcasted_iota(jnp.int32, (META, tok), 0)
    device = dev_ref[...]
    target_seq = device // 2
    lines = [pos_ref[i : i + 1, :] >> 6 for i in range(3)]
    lines += [pos_ref[i : i + 1, :] & 63 for i in range(3)]
    lines += [jnp.where(lane[0:1, :] < count, 1, 0)]
    lines += [target_seq, device - target_seq * 2, slot_ref[...]]
    table = jnp.zeros((META, tok), jnp.int32)
    for i, line in enumerate(lines):
        table = jnp.where(row == i, line, table)
    meta[x, z] = table.astype(jnp.float32)

    values = frames_ref[...].astype(jnp.float32)
    mean_square = jnp.mean(values * values, axis=-1, keepdims=True)
    token = lax.broadcasted_iota(jnp.int32, (part, features), 0) + core * part
    gain = jnp.where(token < count, gain_a_ref[...], gain_v_ref[...])
    normed = (values * lax.rsqrt(mean_square + 1e-06) * gain).astype(jnp.bfloat16)
    for target in range(n_seq):
        stage[target] = normed[:, target * width : (target + 1) * width]
    xbuf[x, z, mine, :] = stage[z]

    pl.semaphore_wait(barrier, n_seq + 1)

    def x1_copy(q, source):
        return pltpu.make_async_remote_copy(
            src_ref=stage.at[peers[q]],
            dst_ref=xbuf.at[x, source, mine],
            send_sem=x1_send.at[q],
            recv_sem=x1_recv.at[q],
            device_id={"seq": peers[q]},
            device_id_type=MESH,
        )

    def m1_copy(q, source):
        return pltpu.make_async_remote_copy(
            src_ref=meta.at[x, z],
            dst_ref=meta.at[x, source],
            send_sem=m1_send.at[q],
            recv_sem=m1_recv.at[q],
            device_id={"seq": peers[q]},
            device_id_type=MESH,
        )

    def x2_copy(q, column):
        return pltpu.make_async_remote_copy(
            src_ref=xbuf.at[x, peers[q], mine],
            dst_ref=xbuf.at[column, peers[q], mine],
            send_sem=x2_send.at[q],
            recv_sem=x2_recv.at[q],
            device_id={"mdl": 1 - x},
            device_id_type=MESH,
        )

    def m2_copy(q, column):
        return pltpu.make_async_remote_copy(
            src_ref=meta.at[x, peers[q]],
            dst_ref=meta.at[column, peers[q]],
            send_sem=m2_send.at[q],
            recv_sem=m2_recv.at[q],
            device_id={"mdl": 1 - x},
            device_id_type=MESH,
        )

    def x3_copy(q, column, half, slot):
        rows = pl.ds(pl.multiple_of(half * part, part), part)
        return pltpu.make_async_remote_copy(
            src_ref=xbuf.at[column, peers[q], mine],
            dst_ref=xbuf.at[column, peers[q], rows],
            send_sem=x3_send.at[slot, q],
            recv_sem=x3_recv.at[slot, q],
            device_id={"sub": 1 - core},
            device_id_type=MESH,
        )

    for q in range(n_seq - 1, 0, -1):
        m1_copy(q, z).start()
        x1_copy(q, z).start()
    m2_copy(0, x).start()
    x2_copy(0, x).start()
    for c in range(early):
        for kind in range(2):
            weight_copy(kind, c, x).start()
    x3_copy(0, x, core, 0).start()

    rows = lax.broadcasted_iota(jnp.int32, (n_seq * tok, tok), 0)

    def place(column, q):
        about = meta[column, peers[q]]
        ints = about.astype(jnp.int32)
        block = jnp.bitwise_xor(ints[7:8, :], z)
        key = jnp.where(ints[8:9, :] == x, block * tok + ints[9:10, :], -1)
        piece = jnp.where(rows == key, 1.0, 0.0).astype(jnp.bfloat16)
        return piece, lax.dot_general(
            piece, about.astype(jnp.bfloat16), (((1,), (1,)), ((), ())), preferred_element_type=jnp.float32
        )

    piece, facts = place(x, 0)
    hot[:, :tok] = piece
    for q in range(1, n_seq):
        m1_copy(q, peers[q]).wait_recv()
        m2_copy(q, x).start()
        piece, more = place(x, q)
        hot[:, q * tok : (q + 1) * tok] = piece
        facts += more
    for q in range(1, n_seq):
        x1_copy(q, peers[q]).wait_recv()
        x2_copy(q, x).start()
        x3_copy(q, x, core, 0).start()
    for c in range(early, chunks):
        for kind in range(2):
            weight_copy(kind, c, x).start()
    for q in range(n_seq):
        m2_copy(q, 1 - x).wait_recv()
        piece, more = place(1 - x, q)
        hot[:, (n_seq + q) * tok : (n_seq + q + 1) * tok] = piece
        facts += more
    for q in range(n_seq):
        x2_copy(q, 1 - x).wait_recv()
        x3_copy(q, 1 - x, core, 1).start()
    for slot, column in enumerate((x, 1 - x)):
        for q in range(n_seq):
            x3_copy(q, column, 1 - core, slot).wait_recv()

    everyone = jnp.concatenate(
        [xbuf[column, peers[q]] for column in (x, 1 - x) for q in range(n_seq)], axis=0
    )
    sorted_rows = jnp.dot(hot[...], everyone, preferred_element_type=jnp.float32)
    is_audio = facts[:, 6:7] > 0.5
    lhs[:, :width] = jnp.where(is_audio, sorted_rows, 0.0).astype(jnp.bfloat16)
    lhs[:, width:] = jnp.where(is_audio, 0.0, sorted_rows).astype(jnp.bfloat16)

    for copy in own_weights:
        copy.wait()

    def part_copy(out_slot, in_slot, c, peer):
        return pltpu.make_async_remote_copy(
            src_ref=outbox.at[out_slot, c],
            dst_ref=inbox.at[in_slot, c],
            send_sem=p_send.at[out_slot, c],
            recv_sem=p_recv.at[in_slot, c],
            device_id={"seq": peer},
            device_id_type=MESH,
        )

    def relay(c):
        part_copy(2, 3, c, peers[1]).wait_recv()
        outbox[1, c] = (far[c] + inbox[3, c].astype(jnp.float32)).astype(jnp.bfloat16)
        part_copy(1, 1, c, peers[2]).start()

    def multiply(c, carry):
        for kind in range(2):
            weight_copy(kind, c, 1 - x).wait_recv()
        cols = pl.ds(pl.multiple_of(c * chunk, chunk), chunk)
        product = jnp.dot(lhs[...], weights[:, cols], preferred_element_type=jnp.float32)
        outbox[0, c] = product[tok : 2 * tok, :].astype(jnp.bfloat16)
        outbox[2, c] = product[3 * tok :, :].astype(jnp.bfloat16)

        @pl.when(jnp.logical_not(inner))
        def _():
            part_copy(2, 3, c, peers[1]).start()
            outbox[1, c] = product[2 * tok : 3 * tok, :].astype(jnp.bfloat16)
            part_copy(1, 1, c, peers[2]).start()
            part_copy(0, 0, c, peers[1]).start()

        @pl.when(inner)
        def _():
            part_copy(2, 2, c, peers[3]).start()
            part_copy(0, 0, c, peers[1]).start()
            far[c] = product[2 * tok : 3 * tok, :]

            @pl.when(c > 0)
            def _():
                relay(c - 1)

        own[c] = product[:tok, :]
        return carry

    lax.fori_loop(0, chunks, multiply, 0)

    lanes = lax.broadcasted_iota(jnp.int32, (tok, HEAD), 1)
    pair = jnp.where(lanes < HEAD // 2, lanes, lanes - HEAD // 2)
    at = [facts[:tok, i : i + 1] * 64.0 + facts[:tok, i + 3 : i + 4] for i in range(3)]
    chosen = jnp.where(pair < HEAD // 8, at[0], jnp.where(pair < HEAD * 5 // 16, at[1], at[2]))
    angles = chosen * freq_ref[...]
    turn[0] = jnp.cos(angles)
    sinus = jnp.sin(angles)
    turn[1] = jnp.where(lanes < HEAD // 2, -sinus, sinus)

    @pl.when(inner)
    def _():
        relay(chunks - 1)

    def finish(c, carry):
        part_copy(0, 0, c, peers[1]).wait_recv()
        part_copy(1, 1, c, peers[2]).wait_recv()

        @pl.when(inner)
        def _():
            part_copy(2, 2, c, peers[3]).wait_recv()
            own[c] = own[c] + inbox[2, c].astype(jnp.float32)

        total = own[c] + inbox[0, c].astype(jnp.float32) + inbox[1, c].astype(jnp.float32)
        for h in range(chunk // HEAD):
            head = total[:, h * HEAD : (h + 1) * HEAD]
            turned = head * turn[0] + pltpu.roll(head, HEAD // 2, 1) * turn[1]
            cols = pl.ds(pl.multiple_of(c * chunk + h * HEAD, HEAD), HEAD)
            out_ref[:, cols] = turned.astype(out_ref.dtype)
        return carry

    lax.fori_loop(0, chunks, finish, 0)

    for q in range(n_seq):
        if q:
            x1_copy(q, z).wait_send()
            m1_copy(q, z).wait_send()
        x2_copy(q, x).wait_send()
        m2_copy(q, x).wait_send()
        x3_copy(q, x, core, 0).wait_send()
        x3_copy(q, 1 - x, core, 1).wait_send()

    def drain(c, carry):
        for kind in range(2):
            weight_copy(kind, c, x).wait_send()
        for slot in range(3):
            part_copy(slot, slot, c, peers[1]).wait_send()
        return carry

    lax.fori_loop(0, chunks, drain, 0)


def exchanged_plan(
    frames, audio_count, pos_ids, gain_audio, gain_video, audio_proj, video_proj, dest_device, dest_slot
):
    n_seq = lax.axis_size("seq")
    tok, features = frames.shape
    deep, columns = audio_proj.shape
    width = features // n_seq
    chunk = next(k for k in (2 * HEAD, HEAD) if columns % k == 0)
    chunks = columns // chunk
    early = min(1, chunks)
    freq = inverse_frequencies()
    freq = jnp.concatenate([freq, freq])[None, :]
    vmem = pl.BlockSpec(memory_space=pltpu.VMEM)
    anywhere = pl.BlockSpec(memory_space=pl.ANY)
    dma = pltpu.SemaphoreType.DMA
    bf16, f32, i32 = jnp.bfloat16, jnp.float32, jnp.int32
    return pl.pallas_call(
        functools.partial(kernel, chunk, early),
        out_shape=jax.ShapeDtypeStruct((tok, columns), bf16),
        in_specs=[anywhere] * 7 + [vmem] + [anywhere] * 2,
        out_specs=vmem,
        scratch_shapes=[
            pltpu.SMEM((1,), i32),
            pltpu.VMEM((tok // 2, features), bf16),
            pltpu.VMEM((3, tok), i32),
            pltpu.VMEM((1, tok), i32),
            pltpu.VMEM((1, tok), i32),
            pltpu.VMEM((1, features), f32),
            pltpu.VMEM((1, features), f32),
            pltpu.VMEM((2, n_seq, tok, width), bf16),
            pltpu.VMEM((n_seq, tok // 2, width), bf16),
            pltpu.VMEM((2, n_seq, META, tok), f32),
            pltpu.VMEM((n_seq * tok, 2 * n_seq * tok), bf16),
            pltpu.VMEM((n_seq * tok, 2 * width), bf16),
            pltpu.VMEM((2 * width, columns), bf16),
            pltpu.VMEM((3, chunks, tok, chunk), bf16),
            pltpu.VMEM((4, chunks, tok, chunk), bf16),
            pltpu.VMEM((chunks, tok, chunk), f32),
            pltpu.VMEM((chunks, tok, chunk), f32),
            pltpu.VMEM((2, tok, HEAD), f32),
            dma((7,)),
        ]
        + [dma((n_seq,))] * 8
        + [dma((2, n_seq))] * 2
        + [dma((2, chunks))] * 2
        + [dma((2,)), dma((3, chunks)), dma((4, chunks))],
        compiler_params=pltpu.CompilerParams(
            collective_id=0, has_side_effects=True, vmem_limit_bytes=60 * 1024 * 1024
        ),
    )(
        audio_count,
        frames,
        pos_ids,
        dest_device[None, :],
        dest_slot[None, :],
        gain_audio[None, :],
        gain_video[None, :],
        freq,
        audio_proj,
        video_proj,
    )


def solution(mesh):
    in_specs = (
        P(("grp", "seq", "mdl"), None),
        P(("grp", "seq", "mdl")),
        P(None, ("grp", "seq", "mdl")),
        P(),
        P(),
        P(("seq", "mdl"), "sub"),
        P(("seq", "mdl"), "sub"),
        P(("grp", "seq", "mdl")),
        P(("grp", "seq", "mdl")),
    )
    out_specs = P(("grp", "seq", "mdl"), "sub")
    paired = (mesh.shape["seq"], mesh.shape["mdl"], mesh.shape["sub"]) == (4, 2, 2)
    plan = exchanged_plan if paired else gathered_plan
    return jax.shard_map(plan, mesh=mesh, in_specs=in_specs, out_specs=out_specs, check_vma=False)
```

time: 68.8 us -> 59.2 us (0.86); the launches traced: 67.7 us -> 59 us
  Pallas kernels: 61.8 us -> 54.7 us
  local copies, waits for them, and re-layouts: 5.14 us -> 3.02 us
    pallas_call x1, Pallas kernels: 61.8 us -> 54.7 us  [exchanged_plan(): pl.pallas_call(functools.partial(kernel, chunk, early), out_shape=jax.Sha...]
    unnamed x17 -> x5, local copies, waits for them, and re-layouts: 5.13 us -> 1.82 us
where the time goes in v2:
time: 59.2 us; the launch traced here: 59 us
  Pallas kernels  54.7 us (92%)
  local copies, waits for them, and re-layouts  3.02 us (5%)
  between operations  0.69 us (1%)
  other arithmetic  0.63 us (1%)
    pallas_call x1, Pallas kernels, exchanged_plan(): pl.pallas_call(functools.partial(kernel, chunk, early), out_shape=jax.Sha...  54.7 us
    unnamed x5, local copies, waits for them, and re-layouts  1.82 us

profile of v2, /device:TPU:0, one launch (start us, length us, event | category | flops | bytes accessed | tf_op | source)
XLA Modules:
  0.0 59.0 jit_solution(13537267376780532918)
XLA Ops:
  0.0 0.0 copy-start
  0.7 0.0 copy-start.1
  0.7 0.6 %maximum_bitcast_fusion.freq_ref = f32[1,128]{1,0:T(1,128)} fusion(f32[64]{0:T(128)S(1)} %multiply_power_fusion), kind=kLoop, calls=%fused_computation | loop fusion | flops 128 | bytes 768 | tf_op jit(solution)/shard_map/broadcast_in_dim | solution.py:449
  1.3 0.0 copy-done
  1.3 0.6 %broadcast_in_dim.17.gain_a_hbm = f32[1,1280]{1,0:T(1,128)} reshape(f32[1280]{0:T(1024)S(1)} %copy-done) | data formatting | bytes 10240 | tf_op jit(solution)/shard_map/broadcast_in_dim | solution.py:493
  1.9 0.0 copy-done.1
  1.9 0.6 %broadcast_in_dim.18.gain_v_hbm = f32[1,1280]{1,0:T(1,128)} reshape(f32[1280]{0:T(1024)S(1)} %copy-done.1) | data formatting | bytes 10240 | tf_op jit(solution)/shard_map/broadcast_in_dim | solution.py:494
  2.5 54.7 %shard_map.91 = bf16[128,1792]{1,0:T(8,128)(2,1)} custom-call(s32[1]{0:T(128)S(6)} %copy.11.count_hbm, bf16[128,1280]{1,0:T(8,128)(2,1)} %frames_hbm.1, s32[3,128]{1,0:T(4,128)} %pos_hbm.1, s32[1,128]{1,0:T(1,128)} %bitcast.4, s32[1,128]{1,0:T(1,128)} %bitcast.5, f32[1,1280]{1,0:T(1,128)} %broadcast_in_dim.17.gain_a_hbm, ...), custom_call_target="tpu_custom_call" | custom-call | tf_op jit(solution)/shard_map/pallas_call | solution.py:454
  57.2 1.8 %copy.12 = bf16[128,1792]{1,0:T(8,128)(2,1)} copy(bf16[128,1792]{1,0:T(8,128)(2,1)} %shard_map.91) | data formatting | bytes 917504
  (1 shorter events, 0.0 us)
Async XLA Ops:
  0.0 1.3 %copy-start = (f32[1280]{0:T(1024)S(1)}, f32[1280]{0:T(1024)}, u32[]{:S(2)}) copy-start(f32[1280]{0:T(1024)} %param.12) | copy-start | bytes 15364
  0.7 1.2 %copy-start.1 = (f32[1280]{0:T(1024)S(1)}, f32[1280]{0:T(1024)}, u32[]{:S(2)}) copy-start(f32[1280]{0:T(1024)} %param.13) | copy-start | bytes 15364

commit v3 on v2

--- a/solution.py
+++ b/solution.py
@@ -1,4 +1,5 @@
 import functools
+import math
 
 import jax
 import jax.numpy as jnp
@@ -104,7 +105,6 @@
     slot_hbm,
     gain_a_hbm,
     gain_v_hbm,
-    freq_ref,
     audio_hbm,
     video_hbm,
     out_ref,
@@ -147,6 +147,7 @@
     z = lax.axis_index("seq")
     x = lax.axis_index("mdl")
     core = lax.axis_index("sub")
+    group = lax.axis_index("grp")
     features = frames_hbm.shape[1]
     tok = frames_hbm.shape[0]
     deep = audio_hbm.shape[0]
@@ -179,6 +180,7 @@
         pl.semaphore_signal(barrier, inc=1, device_id={"seq": peers[q]}, device_id_type=MESH)
     pl.semaphore_signal(barrier, inc=1, device_id={"mdl": 1 - x}, device_id_type=MESH)
     pl.semaphore_signal(barrier, inc=1, device_id={"sub": 1 - core}, device_id_type=MESH)
+    pl.semaphore_signal(barrier, inc=1, device_id={"grp": 1 - group}, device_id_type=MESH)
 
     def weight_rows(kind, column):
         return pl.ds(pl.multiple_of(kind * width + column * deep, 16), deep)
@@ -190,18 +192,95 @@
     for copy in own_weights:
         copy.start()
 
-    def weight_copy(kind, c, column):
+    def weight_copy(c, column):
+        at = weights.at[weight_rows(group, column), pl.ds(pl.multiple_of(c * chunk, chunk), chunk)]
+        return pltpu.make_async_remote_copy(
+            src_ref=weights.at[weight_rows(group, x), pl.ds(pl.multiple_of(c * chunk, chunk), chunk)],
+            dst_ref=at,
+            send_sem=w_send.at[0, c],
+            recv_sem=w_recv.at[0, c],
+            device_id={"mdl": 1 - x},
+            device_id_type=MESH,
+        )
+
+    def weight_pass(c, kind):
         cols = pl.ds(pl.multiple_of(c * chunk, chunk), chunk)
         return pltpu.make_async_remote_copy(
-            src_ref=(audio_hbm, video_hbm)[kind].at[:, cols],
-            dst_ref=weights.at[weight_rows(kind, column), cols],
-            send_sem=w_send.at[kind, c],
-            recv_sem=w_recv.at[kind, c],
+            src_ref=weights.at[weight_rows(group, 1 - x), cols],
+            dst_ref=weights.at[weight_rows(kind, 1 - x), cols],
+            send_sem=w_send.at[1, c],
+            recv_sem=w_recv.at[1, c],
+            device_id={"grp": 1 - group},
+            device_id_type=MESH,
+        )
+
+    def start_weights(first, last):
+        def start(c, carry):
+            weight_copy(c, x).start()
+            return carry
+
+        lax.fori_loop(first, last, start, 0)
+
+    def pass_weights(first, last):
+        def forward(c, carry):
+            weight_copy(c, 1 - x).wait_recv()
+            weight_pass(c, group).start()
+            return carry
+
+        lax.fori_loop(first, last, forward, 0)
+
+    def x1_copy(q, source):
+        return pltpu.make_async_remote_copy(
+            src_ref=stage.at[peers[q]],
+            dst_ref=xbuf.at[x, source, mine],
+            send_sem=x1_send.at[q],
+            recv_sem=x1_recv.at[q],
+            device_id={"seq": peers[q]},
+            device_id_type=MESH,
+        )
+
+    def m1_copy(q, source):
+        return pltpu.make_async_remote_copy(
+            src_ref=meta.at[x, z],
+            dst_ref=meta.at[x, source],
+            send_sem=m1_send.at[q],
+            recv_sem=m1_recv.at[q],
+            device_id={"seq": peers[q]},
+            device_id_type=MESH,
+        )
+
+    def x2_copy(q, column):
+        return pltpu.make_async_remote_copy(
+            src_ref=xbuf.at[x, peers[q], mine],
+            dst_ref=xbuf.at[column, peers[q], mine],
+            send_sem=x2_send.at[q],
+            recv_sem=x2_recv.at[q],
             device_id={"mdl": 1 - x},
             device_id_type=MESH,
         )
 
-    for copy in loads:
+    def m2_copy(q, column):
+        return pltpu.make_async_remote_copy(
+            src_ref=meta.at[x, peers[q]],
+            dst_ref=meta.at[column, peers[q]],
+            send_sem=m2_send.at[q],
+            recv_sem=m2_recv.at[q],
+            device_id={"mdl": 1 - x},
+            device_id_type=MESH,
+        )
+
+    def x3_copy(q, column, half, slot):
+        rows = pl.ds(pl.multiple_of(half * part, part), part)
+        return pltpu.make_async_remote_copy(
+            src_ref=xbuf.at[column, peers[q], mine],
+            dst_ref=xbuf.at[column, peers[q], rows],
+            send_sem=x3_send.at[slot, q],
+            recv_sem=x3_recv.at[slot, q],
+            device_id={"sub": 1 - core},
+            device_id_type=MESH,
+        )
+
+    for copy in loads[3:]:
         copy.wait()
     count = count_ref[0]
     lane = lax.broadcasted_iota(jnp.int32, (META, tok), 1)
@@ -217,77 +296,28 @@
         table = jnp.where(row == i, line, table)
     meta[x, z] = table.astype(jnp.float32)
 
+    pl.semaphore_wait(barrier, n_seq + 2)
+    for q in range(n_seq - 1, 0, -1):
+        m1_copy(q, z).start()
+    m2_copy(0, x).start()
+
+    for copy in loads[:3]:
+        copy.wait()
     values = frames_ref[...].astype(jnp.float32)
     mean_square = jnp.mean(values * values, axis=-1, keepdims=True)
     token = lax.broadcasted_iota(jnp.int32, (part, features), 0) + core * part
-    gain = jnp.where(token < count, gain_a_ref[...], gain_v_ref[...])
+    gain = jnp.where(token < count, gain_a_ref[...].reshape(1, features), gain_v_ref[...].reshape(1, features))
     normed = (values * lax.rsqrt(mean_square + 1e-06) * gain).astype(jnp.bfloat16)
     for target in range(n_seq):
         stage[target] = normed[:, target * width : (target + 1) * width]
+    for q in range(n_seq - 1, 0, -1):
+        x1_copy(q, z).start()
     xbuf[x, z, mine, :] = stage[z]
-
-    pl.semaphore_wait(barrier, n_seq + 1)
-
-    def x1_copy(q, source):
-        return pltpu.make_async_remote_copy(
-            src_ref=stage.at[peers[q]],
-            dst_ref=xbuf.at[x, source, mine],
-            send_sem=x1_send.at[q],
-            recv_sem=x1_recv.at[q],
-            device_id={"seq": peers[q]},
-            device_id_type=MESH,
-        )
-
-    def m1_copy(q, source):
-        return pltpu.make_async_remote_copy(
-            src_ref=meta.at[x, z],
-            dst_ref=meta.at[x, source],
-            send_sem=m1_send.at[q],
-            recv_sem=m1_recv.at[q],
-            device_id={"seq": peers[q]},
-            device_id_type=MESH,
-        )
-
-    def x2_copy(q, column):
-        return pltpu.make_async_remote_copy(
-            src_ref=xbuf.at[x, peers[q], mine],
-            dst_ref=xbuf.at[column, peers[q], mine],
-            send_sem=x2_send.at[q],
-            recv_sem=x2_recv.at[q],
-            device_id={"mdl": 1 - x},
-            device_id_type=MESH,
-        )
-
-    def m2_copy(q, column):
-        return pltpu.make_async_remote_copy(
-            src_ref=meta.at[x, peers[q]],
-            dst_ref=meta.at[column, peers[q]],
-            send_sem=m2_send.at[q],
-            recv_sem=m2_recv.at[q],
-            device_id={"mdl": 1 - x},
-            device_id_type=MESH,
-        )
-
-    def x3_copy(q, column, half, slot):
-        rows = pl.ds(pl.multiple_of(half * part, part), part)
-        return pltpu.make_async_remote_copy(
-            src_ref=xbuf.at[column, peers[q], mine],
-            dst_ref=xbuf.at[column, peers[q], rows],
-            send_sem=x3_send.at[slot, q],
-            recv_sem=x3_recv.at[slot, q],
-            device_id={"sub": 1 - core},
-            device_id_type=MESH,
-        )
-
-    for q in range(n_seq - 1, 0, -1):
-        m1_copy(q, z).start()
-        x1_copy(q, z).start()
-    m2_copy(0, x).start()
     x2_copy(0, x).start()
-    for c in range(early):
-        for kind in range(2):
-            weight_copy(kind, c, x).start()
     x3_copy(0, x, core, 0).start()
+    for copy in own_weights:
+        copy.wait()
+    start_weights(0, early)
 
     rows = lax.broadcasted_iota(jnp.int32, (n_seq * tok, tok), 0)
 
@@ -301,43 +331,42 @@
             piece, about.astype(jnp.bfloat16), (((1,), (1,)), ((), ())), preferred_element_type=jnp.float32
         )
 
-    piece, facts = place(x, 0)
-    hot[:, :tok] = piece
+    def put(column, slot, q):
+        piece, more = place(column, q)
+        hot[:, (slot * n_seq + q) * tok : (slot * n_seq + q + 1) * tok] = piece
+        return more
+
+    facts = put(x, 0, 0)
     for q in range(1, n_seq):
         m1_copy(q, peers[q]).wait_recv()
         m2_copy(q, x).start()
-        piece, more = place(x, q)
-        hot[:, q * tok : (q + 1) * tok] = piece
-        facts += more
+    for q in range(1, n_seq):
+        facts += put(x, 0, q)
     for q in range(1, n_seq):
         x1_copy(q, peers[q]).wait_recv()
         x2_copy(q, x).start()
         x3_copy(q, x, core, 0).start()
-    for c in range(early, chunks):
-        for kind in range(2):
-            weight_copy(kind, c, x).start()
+    start_weights(early, chunks)
     for q in range(n_seq):
         m2_copy(q, 1 - x).wait_recv()
-        piece, more = place(1 - x, q)
-        hot[:, (n_seq + q) * tok : (n_seq + q + 1) * tok] = piece
-        facts += more
+        facts += put(1 - x, 1, q)
+    pass_weights(0, early)
+
+    def column_rows(column):
+        return jnp.concatenate([xbuf[column, peers[q]] for q in range(n_seq)], axis=0)
+
+    split = n_seq * tok
     for q in range(n_seq):
+        x3_copy(q, x, 1 - core, 0).wait_recv()
         x2_copy(q, 1 - x).wait_recv()
         x3_copy(q, 1 - x, core, 1).start()
-    for slot, column in enumerate((x, 1 - x)):
-        for q in range(n_seq):
-            x3_copy(q, column, 1 - core, slot).wait_recv()
-
-    everyone = jnp.concatenate(
-        [xbuf[column, peers[q]] for column in (x, 1 - x) for q in range(n_seq)], axis=0
-    )
-    sorted_rows = jnp.dot(hot[...], everyone, preferred_element_type=jnp.float32)
+    sorted_rows = jnp.dot(hot[:, :split], column_rows(x), preferred_element_type=jnp.float32)
+    for q in range(n_seq):
+        x3_copy(q, 1 - x, 1 - core, 1).wait_recv()
+    sorted_rows += jnp.dot(hot[:, split:], column_rows(1 - x), preferred_element_type=jnp.float32)
     is_audio = facts[:, 6:7] > 0.5
     lhs[:, :width] = jnp.where(is_audio, sorted_rows, 0.0).astype(jnp.bfloat16)
     lhs[:, width:] = jnp.where(is_audio, 0.0, sorted_rows).astype(jnp.bfloat16)
-
-    for copy in own_weights:
-        copy.wait()
 
     def part_copy(out_slot, in_slot, c, peer):
         return pltpu.make_async_remote_copy(
@@ -349,14 +378,22 @@
             device_id_type=MESH,
         )
 
-    def relay(c):
+    def relay(c, carry):
         part_copy(2, 3, c, peers[1]).wait_recv()
         outbox[1, c] = (far[c] + inbox[3, c].astype(jnp.float32)).astype(jnp.bfloat16)
         part_copy(1, 1, c, peers[2]).start()
+        return carry
+
+    def near(c, carry):
+        part_copy(0, 0, c, peers[1]).start()
+        return carry
 
     def multiply(c, carry):
-        for kind in range(2):
-            weight_copy(kind, c, 1 - x).wait_recv()
+        @pl.when(c + early < chunks)
+        def _():
+            pass_weights(c + early, c + early + 1)
+
+        weight_pass(c, 1 - group).wait_recv()
         cols = pl.ds(pl.multiple_of(c * chunk, chunk), chunk)
         product = jnp.dot(lhs[...], weights[:, cols], preferred_element_type=jnp.float32)
         outbox[0, c] = product[tok : 2 * tok, :].astype(jnp.bfloat16)
@@ -367,7 +404,6 @@
             part_copy(2, 3, c, peers[1]).start()
             outbox[1, c] = product[2 * tok : 3 * tok, :].astype(jnp.bfloat16)
             part_copy(1, 1, c, peers[2]).start()
-            part_copy(0, 0, c, peers[1]).start()
 
         @pl.when(inner)
         def _():
@@ -375,27 +411,27 @@
             part_copy(0, 0, c, peers[1]).start()
             far[c] = product[2 * tok : 3 * tok, :]
 
-            @pl.when(c > 0)
-            def _():
-                relay(c - 1)
-
         own[c] = product[:tok, :]
         return carry
 
     lax.fori_loop(0, chunks, multiply, 0)
+
+    @pl.when(inner)
+    def _():
+        lax.fori_loop(0, chunks, relay, 0)
+
+    @pl.when(jnp.logical_not(inner))
+    def _():
+        lax.fori_loop(0, chunks, near, 0)
 
     lanes = lax.broadcasted_iota(jnp.int32, (tok, HEAD), 1)
     pair = jnp.where(lanes < HEAD // 2, lanes, lanes - HEAD // 2)
     at = [facts[:tok, i : i + 1] * 64.0 + facts[:tok, i + 3 : i + 4] for i in range(3)]
     chosen = jnp.where(pair < HEAD // 8, at[0], jnp.where(pair < HEAD * 5 // 16, at[1], at[2]))
-    angles = chosen * freq_ref[...]
+    angles = chosen * jnp.exp(pair.astype(jnp.float32) * (-2.0 / HEAD * math.log(1000000.0)))
     turn[0] = jnp.cos(angles)
     sinus = jnp.sin(angles)
     turn[1] = jnp.where(lanes < HEAD // 2, -sinus, sinus)
-
-    @pl.when(inner)
-    def _():
-        relay(chunks - 1)
 
     def finish(c, carry):
         part_copy(0, 0, c, peers[1]).wait_recv()
@@ -426,8 +462,8 @@
         x3_copy(q, 1 - x, core, 1).wait_send()
 
     def drain(c, carry):
-        for kind in range(2):
-            weight_copy(kind, c, x).wait_send()
+        weight_copy(c, x).wait_send()
+        weight_pass(c, group).wait_send()
         for slot in range(3):
             part_copy(slot, slot, c, peers[1]).wait_send()
         return carry
@@ -444,9 +480,7 @@
     width = features // n_seq
     chunk = next(k for k in (2 * HEAD, HEAD) if columns % k == 0)
     chunks = columns // chunk
-    early = min(1, chunks)
-    freq = inverse_frequencies()
-    freq = jnp.concatenate([freq, freq])[None, :]
+    early = min(2, chunks)
     vmem = pl.BlockSpec(memory_space=pltpu.VMEM)
     anywhere = pl.BlockSpec(memory_space=pl.ANY)
     dma = pltpu.SemaphoreType.DMA
@@ -454,7 +488,7 @@
     return pl.pallas_call(
         functools.partial(kernel, chunk, early),
         out_shape=jax.ShapeDtypeStruct((tok, columns), bf16),
-        in_specs=[anywhere] * 7 + [vmem] + [anywhere] * 2,
+        in_specs=[anywhere] * 9,
         out_specs=vmem,
         scratch_shapes=[
             pltpu.SMEM((1,), i32),
@@ -462,8 +496,8 @@
             pltpu.VMEM((3, tok), i32),
             pltpu.VMEM((1, tok), i32),
             pltpu.VMEM((1, tok), i32),
-            pltpu.VMEM((1, features), f32),
-            pltpu.VMEM((1, features), f32),
+            pltpu.VMEM((features,), f32),
+            pltpu.VMEM((features,), f32),
             pltpu.VMEM((2, n_seq, tok, width), bf16),
             pltpu.VMEM((n_seq, tok // 2, width), bf16),
             pltpu.VMEM((2, n_seq, META, tok), f32),
@@ -490,9 +524,8 @@
         pos_ids,
         dest_device[None, :],
         dest_slot[None, :],
-        gain_audio[None, :],
-        gain_video[None, :],
-        freq,
+        gain_audio,
+        gain_video,
         audio_proj,
         video_proj,
     )

time: 59.2 us -> 55.3 us (0.934)
  Pallas kernels: 54.7 us -> 52.7 us
  local copies, waits for them, and re-layouts: 3.02 us -> 1.82 us
  other arithmetic: 0.63 us -> 0 us
    pallas_call x1, Pallas kernels: 54.7 us -> 52.7 us  [exchanged_plan(): pl.pallas_call(functools.partial(kernel, chunk, early), out_shape=jax.Sha...]
    broadcast_in_dim x2 -> x0, local copies, waits for them, and re-layouts: 1.19 us -> none  [the longest x1 0.6 us: exchanged_plan(): gain_audio[None, :]]
    broadcast_in_dim x1 -> x0, other arithmetic: 0.62 us -> none  [exchanged_plan(): freq = jnp.concatenate([freq, freq])[None, :]]
    unnamed x5 -> x1, local copies, waits for them, and re-layouts: 1.82 us -> 1.82 us
where the time goes in v3:
time: 55.3 us; the launch traced here: 55.2 us
  Pallas kernels  52.7 us (95%)
  local copies, waits for them, and re-layouts  1.82 us (3%)
  between operations  0.66 us (1%)
    pallas_call x1, Pallas kernels, exchanged_plan(): pl.pallas_call(functools.partial(kernel, chunk, early), out_shape=jax.Sha...  52.7 us
    unnamed x1, local copies, waits for them, and re-layouts  1.82 us

profile of v3, /device:TPU:0, one launch (start us, length us, event | category | flops | bytes accessed | tf_op | source)
XLA Modules:
  0.0 55.2 jit_solution(16295217261288970444)
XLA Ops:
  0.7 52.7 %shard_map.91 = bf16[128,1792]{1,0:T(8,128)(2,1)} custom-call(s32[1]{0:T(128)S(6)} %copy.11.count_hbm, bf16[128,1280]{1,0:T(8,128)(2,1)} %frames_hbm.1, s32[3,128]{1,0:T(4,128)} %pos_hbm.1, s32[1,128]{1,0:T(1,128)} %bitcast.2, s32[1,128]{1,0:T(1,128)} %bitcast.3, f32[1280]{0:T(1024)} %gain_a_hbm.1, f32[1280]{0:T(1024)} %gain_v_hbm.1, ...), custom_call_target="tpu_custom_call" | custom-call | tf_op jit(solution)/shard_map/pallas_call | solution.py:488
  53.4 1.8 %copy.12 = bf16[128,1792]{1,0:T(8,128)(2,1)} copy(bf16[128,1792]{1,0:T(8,128)(2,1)} %shard_map.91) | data formatting | bytes 917504

commit v4 on v3

--- a/solution.py
+++ b/solution.py
@@ -107,6 +107,7 @@
     gain_v_hbm,
     audio_hbm,
     video_hbm,
+    out_hbm,
     out_ref,
     count_ref,
     frames_ref,
@@ -142,6 +143,7 @@
     w_own,
     p_send,
     p_recv,
+    out_sem,
 ):
     n_seq = 4
     z = lax.axis_index("seq")
@@ -297,7 +299,7 @@
     meta[x, z] = table.astype(jnp.float32)
 
     pl.semaphore_wait(barrier, n_seq + 2)
-    for q in range(n_seq - 1, 0, -1):
+    for q in range(1, n_seq):
         m1_copy(q, z).start()
     m2_copy(0, x).start()
 
@@ -310,7 +312,7 @@
     normed = (values * lax.rsqrt(mean_square + 1e-06) * gain).astype(jnp.bfloat16)
     for target in range(n_seq):
         stage[target] = normed[:, target * width : (target + 1) * width]
-    for q in range(n_seq - 1, 0, -1):
+    for q in range(1, n_seq):
         x1_copy(q, z).start()
     xbuf[x, z, mine, :] = stage[z]
     x2_copy(0, x).start()
@@ -433,6 +435,10 @@
     sinus = jnp.sin(angles)
     turn[1] = jnp.where(lanes < HEAD // 2, -sinus, sinus)
 
+    def out_copy(c):
+        cols = pl.ds(pl.multiple_of(c * chunk, chunk), chunk)
+        return pltpu.make_async_copy(out_ref.at[:, cols], out_hbm.at[:, cols], out_sem.at[c])
+
     def finish(c, carry):
         part_copy(0, 0, c, peers[1]).wait_recv()
         part_copy(1, 1, c, peers[2]).wait_recv()
@@ -448,6 +454,7 @@
             turned = head * turn[0] + pltpu.roll(head, HEAD // 2, 1) * turn[1]
             cols = pl.ds(pl.multiple_of(c * chunk + h * HEAD, HEAD), HEAD)
             out_ref[:, cols] = turned.astype(out_ref.dtype)
+        out_copy(c).start()
         return carry
 
     lax.fori_loop(0, chunks, finish, 0)
@@ -464,6 +471,7 @@
     def drain(c, carry):
         weight_copy(c, x).wait_send()
         weight_pass(c, group).wait_send()
+        out_copy(c).wait()
         for slot in range(3):
             part_copy(slot, slot, c, peers[1]).wait_send()
         return carry
@@ -481,7 +489,6 @@
     chunk = next(k for k in (2 * HEAD, HEAD) if columns % k == 0)
     chunks = columns // chunk
     early = min(2, chunks)
-    vmem = pl.BlockSpec(memory_space=pltpu.VMEM)
     anywhere = pl.BlockSpec(memory_space=pl.ANY)
     dma = pltpu.SemaphoreType.DMA
     bf16, f32, i32 = jnp.bfloat16, jnp.float32, jnp.int32
@@ -489,8 +496,9 @@
         functools.partial(kernel, chunk, early),
         out_shape=jax.ShapeDtypeStruct((tok, columns), bf16),
         in_specs=[anywhere] * 9,
-        out_specs=vmem,
+        out_specs=anywhere,
         scratch_shapes=[
+            pltpu.VMEM((tok, columns), bf16),
             pltpu.SMEM((1,), i32),
             pltpu.VMEM((tok // 2, features), bf16),
             pltpu.VMEM((3, tok), i32),
@@ -514,7 +522,7 @@
         + [dma((n_seq,))] * 8
         + [dma((2, n_seq))] * 2
         + [dma((2, chunks))] * 2
-        + [dma((2,)), dma((3, chunks)), dma((4, chunks))],
+        + [dma((2,)), dma((3, chunks)), dma((4, chunks)), dma((chunks,))],
         compiler_params=pltpu.CompilerParams(
             collective_id=0, has_side_effects=True, vmem_limit_bytes=60 * 1024 * 1024
         ),

time: 55.3 us -> 54.9 us (level)
  no operation moved by 1% of the time
where the time goes in v4:
time: 54.9 us; the launch traced here: 54.7 us
  Pallas kernels  52.3 us (95%)
  local copies, waits for them, and re-layouts  1.82 us (3%)
  between operations  0.66 us (1%)
    pallas_call x1, Pallas kernels, exchanged_plan(): pl.pallas_call(functools.partial(kernel, chunk, early), out_shape=jax.Sha...  52.3 us
    unnamed x1, local copies, waits for them, and re-layouts  1.82 us

profile of v4, /device:TPU:0, one launch (start us, length us, event | category | flops | bytes accessed | tf_op | source)
XLA Modules:
  0.0 54.7 jit_solution(15203325990481981786)
XLA Ops:
  0.7 52.3 %shard_map.91 = bf16[128,1792]{1,0:T(8,128)(2,1)} custom-call(s32[1]{0:T(128)S(6)} %copy.11.count_hbm, bf16[128,1280]{1,0:T(8,128)(2,1)} %frames_hbm.1, s32[3,128]{1,0:T(4,128)} %pos_hbm.1, s32[1,128]{1,0:T(1,128)} %bitcast.2, s32[1,128]{1,0:T(1,128)} %bitcast.3, f32[1280]{0:T(1024)} %gain_a_hbm.1, f32[1280]{0:T(1024)} %gain_v_hbm.1, ...), custom_call_target="tpu_custom_call" | custom-call | tf_op jit(solution)/shard_map/pallas_call | solution.py:495
  52.9 1.8 %copy.12 = bf16[128,1792]{1,0:T(8,128)(2,1)} copy(bf16[128,1792]{1,0:T(8,128)(2,1)} %shard_map.91) | data formatting | bytes 917504
